TPU v7x, 256 devices: a whole 4x4x8 slice. The times are simulated.
256 devices in a mesh: grp: 8 (over x, y_hi), blk: 32 (over z, y_lo, core).
Axes of the slice: x: 4, y: 4 (y_hi: 2, y_lo: 2; y = y_hi * 2 + y_lo), z: 8, core: 2. Of those that a mesh axis runs over, the one named last changes fastest.
Arguments:
- counts: int32 [65536, 1024], P(('grp', 'blk')), may hold values from 0 to 5
- tile_live: int32 [512, 8], P(('grp', 'blk')), may hold values from 0 to 1
- doc_lengths: int32 [65536], P(('grp', 'blk')), may hold values from 256 to 4095
- doc_mix: bfloat16 [65536, 4096], P(('grp', 'blk')), may hold values from 0.019897461 to 50
- word_topic: float32 [4096, 4096], P('blk'), may hold values from 0.01 to 8
- topic_total: float32 [4096], replicated, may hold values from 20000 to 400000
Outputs:
- doc_share: bfloat16 [65536, 4096], P(('grp', 'blk'))
- word_topic_new: float32 [4096, 4096], P('blk')
- topic_mean: float32 [4096], replicated
All inputs are finite; a program needn't handle non-finite values.
Results may differ from a plain program's by a relative error of at most 0.0004.
The roundings to bfloat16 on the way count: a program that leaves them out, or rounds other values in their place, can miss the bound.
Values may be sent and summed in bfloat16 or wider, within the bound.
A program may use at most 128 MiB of HBM per device.

v0:
```python
import jax
import jax.numpy as jnp
from jax import lax
from jax.sharding import PartitionSpec as P

VOCAB = 262144
alpha_prior = 0.1
beta_prior = 0.01


def passed_along(block, axis, distance):
    devices = range(lax.axis_size(axis))
    route = [((i - distance) % len(devices), i) for i in devices]
    return lax.ppermute(block, axis, route)


def tile_terms(operands):
    doc_rows, block_counts, visitor = operands
    normalizer = jnp.dot(doc_rows, visitor.T, preferred_element_type=jnp.float32)
    ratio = (block_counts / normalizer).astype(jnp.bfloat16)
    doc_part = jnp.dot(ratio, visitor, preferred_element_type=jnp.float32)
    word_part = jnp.dot(ratio.T, doc_rows, preferred_element_type=jnp.float32)
    return (doc_part, word_part)


def shard_terms(visitor, block_counts, doc_low):
    return tile_terms((doc_low, block_counts, visitor))


def local(counts, tile_live, doc_lengths, doc_mix, word_topic, topic_total):
    block_rows = word_topic.shape[0]
    visits = tile_live.shape[1]
    word_weight = (word_topic + beta_prior) / (topic_total + beta_prior * VOCAB)[None, :]
    word_low = word_weight.astype(jnp.bfloat16)
    mix_wide = doc_mix.astype(jnp.float32)
    doc_theta = mix_wide / jnp.sum(mix_wide, axis=1, keepdims=True)
    doc_weight = doc_lengths.astype(jnp.float32)[:, None] * doc_theta + alpha_prior
    doc_low = doc_weight.astype(jnp.bfloat16)
    live_full = jnp.repeat(jnp.repeat(tile_live, block_rows, axis=0), block_rows, axis=1)
    live_counts = counts.astype(jnp.float32) * live_full.astype(jnp.float32)
    window_len = jnp.sum(live_counts, axis=1)
    doc_proj = jnp.zeros((doc_low.shape[0], doc_low.shape[1]), jnp.float32)
    word_accum = jnp.zeros((block_rows, doc_low.shape[1]), jnp.float32)
    visitor = word_low
    for offset in range(visits):
        if offset > 0:
            visitor, word_accum = (
                passed_along(visitor.astype(jnp.float32), "blk", -1).astype(visitor.dtype),
                passed_along(word_accum, "blk", -1),
            )
        block_counts = live_counts[:, offset * block_rows : (offset + 1) * block_rows]
        doc_part, word_part = shard_terms(visitor, block_counts, doc_low)
        doc_proj = doc_proj + doc_part
        word_accum = word_accum + word_part
    word_accum = passed_along(word_accum, "blk", visits - 1)
    doc_new = doc_weight * doc_proj
    column_sum = jnp.sum(doc_new, axis=0)
    topic_count = doc_low.shape[1]
    doc_share = (
        topic_count * (doc_new + alpha_prior) / (window_len[:, None] + topic_count * alpha_prior)
    ).astype(jnp.bfloat16)
    word_sum = lax.psum(word_accum, "grp")
    topic_sum = lax.psum(column_sum, ("grp", "blk"))
    vocab_window = block_rows * lax.axis_size("blk")
    return (doc_share, word_weight * word_sum, topic_sum / vocab_window)


def solution(mesh):
    return jax.shard_map(
        local,
        mesh=mesh,
        in_specs=(
            P(("grp", "blk"), None),
            P(("grp", "blk"), None),
            P(("grp", "blk")),
            P(("grp", "blk"), None),
            P("blk", None),
            P(),
        ),
        out_specs=(P(("grp", "blk"), None), P("blk", None), P()),
        check_vma=False,
    )
```

profile of v0, /device:TPU:161, one launch (start us, length us, event | category | flops | bytes accessed | tf_op | source)
XLA Modules:
  0.0 519.2 jit_solution(7656554678656352072)
XLA Ops:
  7.2 0.8 convert_element_type.95
  8.1 2.0 convert_reduce_fusion
  10.0 0.7 broadcast_add_fusion
  10.7 1.0 fusion.8
  12.4 1.0 copy-done
  13.7 0.7 fusion.9
  14.8 0.8 collective-permute-start.7
  15.6 1.5 collective-permute-start
  17.1 34.7 %collective-permute-done = bf16[128,4096]{1,0:T(8,128)(2,1)S(1)} collective-permute-done((bf16[128,4096]{1,0:T(8,128)(2,1)S(1)}, bf16[128,4096]{1,0:T(8,128)(2,1)S(1)}, u32[]{:S(2)}, u32[]{:S(2)}) %collective-permute-start) | collective-permute-done | bytes 1048608 | tf_op jit(solution)/shard_map/ppermute | solution.py:14
  51.7 0.7 fusion.10
  52.5 0.5 convolution_add_fusion.2
  53.2 2.8 collective-permute-start.1
  56.0 33.8 %collective-permute-done.1 = bf16[128,4096]{1,0:T(8,128)(2,1)S(1)} collective-permute-done((bf16[128,4096]{1,0:T(8,128)(2,1)S(1)}, bf16[128,4096]{1,0:T(8,128)(2,1)S(1)}, u32[]{:S(2)}, u32[]{:S(2)}) %collective-permute-start.1) | collective-permute-done | bytes 1048608 | tf_op jit(solution)/shard_map/ppermute | solution.py:14
  89.8 0.7 fusion.11
  90.5 0.5 fusion.42
  91.3 1.1 collective-permute-start.9
  92.4 2.8 collective-permute-start.2
  95.2 32.9 %collective-permute-done.2 = bf16[128,4096]{1,0:T(8,128)(2,1)S(1)} collective-permute-done((bf16[128,4096]{1,0:T(8,128)(2,1)S(1)}, bf16[128,4096]{1,0:T(8,128)(2,1)S(1)}, u32[]{:S(2)}, u32[]{:S(2)}) %collective-permute-start.2) | collective-permute-done | bytes 1048608 | tf_op jit(solution)/shard_map/ppermute | solution.py:14
  128.0 0.7 fusion.12
  129.5 2.0 collective-permute-start.10
  131.5 2.8 collective-permute-start.3
  134.3 32.0 %collective-permute-done.3 = bf16[128,4096]{1,0:T(8,128)(2,1)S(1)} collective-permute-done((bf16[128,4096]{1,0:T(8,128)(2,1)S(1)}, bf16[128,4096]{1,0:T(8,128)(2,1)S(1)}, u32[]{:S(2)}, u32[]{:S(2)}) %collective-permute-start.3) | collective-permute-done | bytes 1048608 | tf_op jit(solution)/shard_map/ppermute | solution.py:14
  166.3 0.7 fusion.13
  167.7 2.9 collective-permute-start.11
  170.6 2.8 collective-permute-start.4
  173.4 31.1 %collective-permute-done.4 = bf16[128,4096]{1,0:T(8,128)(2,1)S(1)} collective-permute-done((bf16[128,4096]{1,0:T(8,128)(2,1)S(1)}, bf16[128,4096]{1,0:T(8,128)(2,1)S(1)}, u32[]{:S(2)}, u32[]{:S(2)}) %collective-permute-start.4) | collective-permute-done | bytes 1048608 | tf_op jit(solution)/shard_map/ppermute | solution.py:14
  204.5 0.7 fusion.14
  206.0 3.8 collective-permute-start.12
  209.8 2.8 collective-permute-start.5
  212.6 30.2 %collective-permute-done.5 = bf16[128,4096]{1,0:T(8,128)(2,1)S(1)} collective-permute-done((bf16[128,4096]{1,0:T(8,128)(2,1)S(1)}, bf16[128,4096]{1,0:T(8,128)(2,1)S(1)}, u32[]{:S(2)}, u32[]{:S(2)}) %collective-permute-start.5) | collective-permute-done | bytes 1048608 | tf_op jit(solution)/shard_map/ppermute | solution.py:14
  242.7 0.7 fusion.15
  244.2 4.7 collective-permute-start.13
  248.9 2.8 collective-permute-start.6
  251.7 0.7 fusion.40
  252.4 28.6 %collective-permute-done.6 = bf16[128,4096]{1,0:T(8,128)(2,1)S(1)} collective-permute-done((bf16[128,4096]{1,0:T(8,128)(2,1)S(1)}, bf16[128,4096]{1,0:T(8,128)(2,1)S(1)}, u32[]{:S(2)}, u32[]{:S(2)}) %collective-permute-start.6) | collective-permute-done | bytes 1048608 | tf_op jit(solution)/shard_map/ppermute | solution.py:14
  281.0 0.7 fusion.16
  282.4 6.9 %collective-permute-start.14 = (f32[128,4096]{1,0:T(8,128)S(1)}, f32[128,4096]{1,0:T(8,128)}, u32[]{:S(2)}, u32[]{:S(2)}) collective-permute-start(f32[128,4096]{1,0:T(8,128)S(1)} %add.96), channel_id=1, source_target_pairs={{25,0},{26,1},{27,2},{28,3},{29,4},{30,5},{31,6},{0,7},{1,8},{2,9}... | collective-permute-start | bytes 6291464 | tf_op jit(solution)/shard_map/ppermute | solution.py:14
  289.3 2.7 convolution_add_fusion.1
  292.0 2.6 fusion.52
  294.6 2.6 fusion.51
  297.2 2.7 fusion.50
  299.9 2.7 fusion.49
  302.6 2.6 fusion.48
  305.2 69.0 %collective-permute-done.14 = f32[128,4096]{1,0:T(8,128)} collective-permute-done((f32[128,4096]{1,0:T(8,128)S(1)}, f32[128,4096]{1,0:T(8,128)}, u32[]{:S(2)}, u32[]{:S(2)}) %collective-permute-start.14) | collective-permute-done | bytes 2097184 | tf_op jit(solution)/shard_map/ppermute | solution.py:14
  374.2 11.5 %fusion.39 = (f32[4096]{0:T(1024)S(1)}, bf16[256,4096]{1,0:T(8,128)(2,1)}) fusion(f32[256]{0:T(256)S(1)} %broadcast_add_fusion.1, f32[256,4096]{1,0:T(8,128)} %fusion.48, f32[256,4096]{1,0:T(8,128)} %fusion.49, f32[256,4096]{1,0:T(8,128)} %fusion.50, f32[256,4096]{1,0:T(8,128)} %fusion.51, f32[256,4096]{1,0:T(8,128)} %fusion.52, ...), kind=kOutput, calls=%fused_computation.64 | convolution fusion | flops 285208576 | bytes 30493696 | tf_op jit(solution)/shard_map/dot_general | solution.py:21
  385.7 122.8 %psum.15 = f32[4096]{0:T(1024)S(1)} all-reduce(f32[4096]{0:T(1024)S(1)} %get-tuple-element.5), channel_id=1, replica_groups=mesh['grp'=8,'blk'=32] {'grp','blk'}, use_global_device_ids=true, to_apply=%region_4.0 | all-reduce | flops 4096 | bytes 32768 | tf_op jit(solution)/shard_map/psum | solution.py:63
  508.5 0.6 broadcast_multiply_fusion
  509.1 3.2 fusion.17
  (36 shorter events, 5.5 us)
Async XLA Ops:
  7.2 3.6 copy-start.1
  7.2 2.8 copy-start.3
  7.2 501.9 %all-reduce.2.cloned.1.call-start = ((), (), s32[]{:S(2)}) async-start(), calls=%async_computation | async-start | bytes 4194304 | tf_op jit(solution)/shard_map/psum | solution.py:62
  10.7 1.4 copy-start.2
  11.8 1.6 copy-start
  14.8 37.6 %collective-permute-start.7 = (f32[128,4096]{1,0:T(8,128)S(1)}, f32[128,4096]{1,0:T(8,128)S(1)}, u32[]{:S(2)}, u32[]{:S(2)}) collective-permute-start(f32[128,4096]{1,0:T(8,128)S(1)} %fusion.41), channel_id=1, source_target_pairs={{1,0},{2,1},{3,2},{4,3},{5,4},{6,5},{7,6},{8,7},{9,8},{10,9},{11,1... | collective-permute-start | bytes 6291464 | tf_op jit(solution)/shard_map/ppermute | solution.py:14
  15.6 36.1 %collective-permute-start = (bf16[128,4096]{1,0:T(8,128)(2,1)S(1)}, bf16[128,4096]{1,0:T(8,128)(2,1)S(1)}, u32[]{:S(2)}, u32[]{:S(2)}) collective-permute-start(bf16[128,4096]{1,0:T(8,128)(2,1)S(1)} %fusion.18), channel_id=1, source_target_pairs={{1,0},{2,1},{3,2},{4,3},{5,4},{6,5},{7,6},{8,7},{9,8},{10,9},{11,1... | collective-permute-start | bytes 3145736 | tf_op jit(solution)/shard_map/ppermute | solution.py:14
  53.0 38.0 %collective-permute-start.8 = (f32[128,4096]{1,0:T(8,128)S(1)}, f32[128,4096]{1,0:T(8,128)S(1)}, u32[]{:S(2)}, u32[]{:S(2)}) collective-permute-start(f32[128,4096]{1,0:T(8,128)S(1)} %convolution_add_fusion.2), channel_id=1, source_target_pairs={{1,0},{2,1},{3,2},{4,3},{5,4},{6,5},{7,6},{8,7},{9,8},{10,9},{11,1... | collective-permute-start | bytes 6291464 | tf_op jit(solution)/shard_map/ppermute | solution.py:14
  53.2 36.6 %collective-permute-start.1 = (bf16[128,4096]{1,0:T(8,128)(2,1)S(1)}, bf16[128,4096]{1,0:T(8,128)(2,1)S(1)}, u32[]{:S(2)}, u32[]{:S(2)}) collective-permute-start(bf16[128,4096]{1,0:T(8,128)(2,1)S(1)} %collective-permute-done), channel_id=1, source_target_pairs={{1,0},{2,1},{3,2},{4,3},{5,4},{6,5},{7,6},{8,7},{9,8},{10,9},{11,1... | collective-permute-start | bytes 3145736 | tf_op jit(solution)/shard_map/ppermute | solution.py:14
  91.3 38.0 %collective-permute-start.9 = (f32[128,4096]{1,0:T(8,128)S(1)}, f32[128,4096]{1,0:T(8,128)S(1)}, u32[]{:S(2)}, u32[]{:S(2)}) collective-permute-start(f32[128,4096]{1,0:T(8,128)S(1)} %add.91), channel_id=1, source_target_pairs={{1,0},{2,1},{3,2},{4,3},{5,4},{6,5},{7,6},{8,7},{9,8},{10,9},{11,1... | collective-permute-start | bytes 6291464 | tf_op jit(solution)/shard_map/ppermute | solution.py:14
  92.4 35.7 %collective-permute-start.2 = (bf16[128,4096]{1,0:T(8,128)(2,1)S(1)}, bf16[128,4096]{1,0:T(8,128)(2,1)S(1)}, u32[]{:S(2)}, u32[]{:S(2)}) collective-permute-start(bf16[128,4096]{1,0:T(8,128)(2,1)S(1)} %collective-permute-done.1), channel_id=1, source_target_pairs={{1,0},{2,1},{3,2},{4,3},{5,4},{6,5},{7,6},{8,7},{9,8},{10,9},{11,1... | collective-permute-start | bytes 3145736 | tf_op jit(solution)/shard_map/ppermute | solution.py:14
  129.5 38.0 %collective-permute-start.10 = (f32[128,4096]{1,0:T(8,128)S(1)}, f32[128,4096]{1,0:T(8,128)S(1)}, u32[]{:S(2)}, u32[]{:S(2)}) collective-permute-start(f32[128,4096]{1,0:T(8,128)S(1)} %add.92), channel_id=1, source_target_pairs={{1,0},{2,1},{3,2},{4,3},{5,4},{6,5},{7,6},{8,7},{9,8},{10,9},{11,1... | collective-permute-start | bytes 6291464 | tf_op jit(solution)/shard_map/ppermute | solution.py:14
  131.5 34.8 %collective-permute-start.3 = (bf16[128,4096]{1,0:T(8,128)(2,1)S(1)}, bf16[128,4096]{1,0:T(8,128)(2,1)S(1)}, u32[]{:S(2)}, u32[]{:S(2)}) collective-permute-start(bf16[128,4096]{1,0:T(8,128)(2,1)S(1)} %collective-permute-done.2), channel_id=1, source_target_pairs={{1,0},{2,1},{3,2},{4,3},{5,4},{6,5},{7,6},{8,7},{9,8},{10,9},{11,1... | collective-permute-start | bytes 3145736 | tf_op jit(solution)/shard_map/ppermute | solution.py:14
  167.7 38.0 %collective-permute-start.11 = (f32[128,4096]{1,0:T(8,128)S(1)}, f32[128,4096]{1,0:T(8,128)S(1)}, u32[]{:S(2)}, u32[]{:S(2)}) collective-permute-start(f32[128,4096]{1,0:T(8,128)S(1)} %add.93), channel_id=1, source_target_pairs={{1,0},{2,1},{3,2},{4,3},{5,4},{6,5},{7,6},{8,7},{9,8},{10,9},{11,1... | collective-permute-start | bytes 6291464 | tf_op jit(solution)/shard_map/ppermute | solution.py:14
  170.6 33.9 %collective-permute-start.4 = (bf16[128,4096]{1,0:T(8,128)(2,1)S(1)}, bf16[128,4096]{1,0:T(8,128)(2,1)S(1)}, u32[]{:S(2)}, u32[]{:S(2)}) collective-permute-start(bf16[128,4096]{1,0:T(8,128)(2,1)S(1)} %collective-permute-done.3), channel_id=1, source_target_pairs={{1,0},{2,1},{3,2},{4,3},{5,4},{6,5},{7,6},{8,7},{9,8},{10,9},{11,1... | collective-permute-start | bytes 3145736 | tf_op jit(solution)/shard_map/ppermute | solution.py:14
  206.0 38.0 %collective-permute-start.12 = (f32[128,4096]{1,0:T(8,128)S(1)}, f32[128,4096]{1,0:T(8,128)S(1)}, u32[]{:S(2)}, u32[]{:S(2)}) collective-permute-start(f32[128,4096]{1,0:T(8,128)S(1)} %add.94), channel_id=1, source_target_pairs={{1,0},{2,1},{3,2},{4,3},{5,4},{6,5},{7,6},{8,7},{9,8},{10,9},{11,1... | collective-permute-start | bytes 6291464 | tf_op jit(solution)/shard_map/ppermute | solution.py:14
  209.8 33.0 %collective-permute-start.5 = (bf16[128,4096]{1,0:T(8,128)(2,1)S(1)}, bf16[128,4096]{1,0:T(8,128)(2,1)S(1)}, u32[]{:S(2)}, u32[]{:S(2)}) collective-permute-start(bf16[128,4096]{1,0:T(8,128)(2,1)S(1)} %collective-permute-done.4), channel_id=1, source_target_pairs={{1,0},{2,1},{3,2},{4,3},{5,4},{6,5},{7,6},{8,7},{9,8},{10,9},{11,1... | collective-permute-start | bytes 3145736 | tf_op jit(solution)/shard_map/ppermute | solution.py:14
  244.2 38.0 %collective-permute-start.13 = (f32[128,4096]{1,0:T(8,128)S(1)}, f32[128,4096]{1,0:T(8,128)S(1)}, u32[]{:S(2)}, u32[]{:S(2)}) collective-permute-start(f32[128,4096]{1,0:T(8,128)S(1)} %add.95), channel_id=1, source_target_pairs={{1,0},{2,1},{3,2},{4,3},{5,4},{6,5},{7,6},{8,7},{9,8},{10,9},{11,1... | collective-permute-start | bytes 6291464 | tf_op jit(solution)/shard_map/ppermute | solution.py:14
  248.9 32.1 %collective-permute-start.6 = (bf16[128,4096]{1,0:T(8,128)(2,1)S(1)}, bf16[128,4096]{1,0:T(8,128)(2,1)S(1)}, u32[]{:S(2)}, u32[]{:S(2)}) collective-permute-start(bf16[128,4096]{1,0:T(8,128)(2,1)S(1)} %collective-permute-done.5), channel_id=1, source_target_pairs={{1,0},{2,1},{3,2},{4,3},{5,4},{6,5},{7,6},{8,7},{9,8},{10,9},{11,1... | collective-permute-start | bytes 3145736 | tf_op jit(solution)/shard_map/ppermute | solution.py:14
  282.4 91.8 %collective-permute-start.14 = (f32[128,4096]{1,0:T(8,128)S(1)}, f32[128,4096]{1,0:T(8,128)}, u32[]{:S(2)}, u32[]{:S(2)}) collective-permute-start(f32[128,4096]{1,0:T(8,128)S(1)} %add.96), channel_id=1, source_target_pairs={{25,0},{26,1},{27,2},{28,3},{29,4},{30,5},{31,6},{0,7},{1,8},{2,9}... | collective-permute-start | bytes 6291464 | tf_op jit(solution)/shard_map/ppermute | solution.py:14
Sparse Core Ops, SparseCore 0:
  374.3 117.2 all-reduce.1
where the time goes:
time: 520 us; the launch traced here: 519 us
  waiting for transfers between devices  292 us (56%)
  blocking collectives  123 us (24%)
  starting transfers between devices  40.6 us (8%)
  matrix products  37.6 us (7%)
  between operations  14.3 us (3%)
  other arithmetic  10.4 us (2%)
    ppermute x15, waiting for transfers between devices, passed_along(): return lax.ppermute(block, axis, route)  292 us
    psum x1, blocking collectives, local(): topic_sum = lax.psum(column_sum, ('grp', 'blk'))  123 us
    ppermute x15, starting transfers between devices, passed_along(): return lax.ppermute(block, axis, route)  40.6 us
    dot_general x8, matrix products, tile_terms(): doc_part = jnp.dot(ratio, visitor, preferred_element_type=jnp.float32)  28.1 us
  transfers between devices with their start and end apart: 16, of which 8 were waited for; matrix products, arithmetic and copies ran while one was open for 7% of the time, Pallas kernels for 0%

commit v1 on v0

--- a/solution.py
+++ b/solution.py
@@ -6,6 +6,7 @@
 VOCAB = 262144
 alpha_prior = 0.1
 beta_prior = 0.01
+turn_threads = lambda slab_in: lax.psum(lax.psum(slab_in, "grp"), "blk")
 
 
 def passed_along(block, axis, distance):
@@ -60,7 +61,7 @@
         topic_count * (doc_new + alpha_prior) / (window_len[:, None] + topic_count * alpha_prior)
     ).astype(jnp.bfloat16)
     word_sum = lax.psum(word_accum, "grp")
-    topic_sum = lax.psum(column_sum, ("grp", "blk"))
+    topic_sum = turn_threads(column_sum)
     vocab_window = block_rows * lax.axis_size("blk")
     return (doc_share, word_weight * word_sum, topic_sum / vocab_window)
 

time: 520 us -> 548 us (1.054)
  the two profiles are of different devices: /device:TPU:161 before, /device:TPU:0 now
where the time goes in v1:
time: 548 us
  waiting for transfers between devices  294 us (54%)
  blocking collectives  159 us (29%)
  matrix products  37.6 us (7%)
  starting transfers between devices  31 us (6%)
  between operations  14.3 us (3%)
  other arithmetic  10.4 us (2%)
    ppermute x15, waiting for transfers between devices, passed_along(): return lax.ppermute(block, axis, route)  294 us
    psum x2, blocking collectives, turn_threads = lambda slab_in: lax.psum(lax.psum(slab_in, 'grp'), 'blk')  159 us
    ppermute x15, starting transfers between devices, passed_along(): return lax.ppermute(block, axis, route)  31 us
    dot_general x8, matrix products, tile_terms(): doc_part = jnp.dot(ratio, visitor, preferred_element_type=jnp.float32)  28.1 us
  transfers between devices with their start and end apart: 16, of which 8 were waited for; matrix products, arithmetic and copies ran while one was open for 7% of the time, Pallas kernels for 0%

profile of v1, /device:TPU:0, one launch (start us, length us, event | category | flops | bytes accessed | tf_op | source)
XLA Modules:
  0.0 547.8 jit_solution(11739202382619594094)
XLA Ops:
  7.2 0.8 convert_element_type.95
  8.1 2.0 convert_reduce_fusion
  10.0 0.7 broadcast_add_fusion
  10.7 1.0 fusion.8
  12.4 1.0 copy-done
  13.7 0.7 fusion.9
  14.4 0.5 fusion.41
  14.9 4.7 collective-permute-start.7
  19.5 0.7 collective-permute-start
  20.2 34.1 %collective-permute-done = bf16[128,4096]{1,0:T(8,128)(2,1)S(1)} collective-permute-done((bf16[128,4096]{1,0:T(8,128)(2,1)S(1)}, bf16[128,4096]{1,0:T(8,128)(2,1)S(1)}, u32[]{:S(2)}, u32[]{:S(2)}) %collective-permute-start) | collective-permute-done | bytes 1048608 | tf_op jit(solution)/shard_map/ppermute | solution.py:15
  54.3 0.7 fusion.10
  55.0 0.5 convolution_add_fusion.2
  55.6 4.1 collective-permute-start.8
  59.8 34.7 %collective-permute-done.1 = bf16[128,4096]{1,0:T(8,128)(2,1)S(1)} collective-permute-done((bf16[128,4096]{1,0:T(8,128)(2,1)S(1)}, bf16[128,4096]{1,0:T(8,128)(2,1)S(1)}, u32[]{:S(2)}, u32[]{:S(2)}) %collective-permute-start.1) | collective-permute-done | bytes 1048608 | tf_op jit(solution)/shard_map/ppermute | solution.py:15
  94.5 0.7 fusion.11
  95.2 0.5 fusion.42
  95.9 4.1 collective-permute-start.9
  100.1 34.7 %collective-permute-done.2 = bf16[128,4096]{1,0:T(8,128)(2,1)S(1)} collective-permute-done((bf16[128,4096]{1,0:T(8,128)(2,1)S(1)}, bf16[128,4096]{1,0:T(8,128)(2,1)S(1)}, u32[]{:S(2)}, u32[]{:S(2)}) %collective-permute-start.2) | collective-permute-done | bytes 1048608 | tf_op jit(solution)/shard_map/ppermute | solution.py:15
  134.8 0.7 fusion.12
  135.5 0.5 fusion.43
  136.3 4.1 collective-permute-start.10
  140.7 34.5 %collective-permute-done.3 = bf16[128,4096]{1,0:T(8,128)(2,1)S(1)} collective-permute-done((bf16[128,4096]{1,0:T(8,128)(2,1)S(1)}, bf16[128,4096]{1,0:T(8,128)(2,1)S(1)}, u32[]{:S(2)}, u32[]{:S(2)}) %collective-permute-start.3) | collective-permute-done | bytes 1048608 | tf_op jit(solution)/shard_map/ppermute | solution.py:15
  175.2 0.7 fusion.13
  175.9 0.5 fusion.44
  176.6 4.1 collective-permute-start.11
  180.8 34.7 %collective-permute-done.4 = bf16[128,4096]{1,0:T(8,128)(2,1)S(1)} collective-permute-done((bf16[128,4096]{1,0:T(8,128)(2,1)S(1)}, bf16[128,4096]{1,0:T(8,128)(2,1)S(1)}, u32[]{:S(2)}, u32[]{:S(2)}) %collective-permute-start.4) | collective-permute-done | bytes 1048608 | tf_op jit(solution)/shard_map/ppermute | solution.py:15
  215.5 0.7 fusion.14
  217.0 4.1 collective-permute-start.12
  221.2 34.7 %collective-permute-done.5 = bf16[128,4096]{1,0:T(8,128)(2,1)S(1)} collective-permute-done((bf16[128,4096]{1,0:T(8,128)(2,1)S(1)}, bf16[128,4096]{1,0:T(8,128)(2,1)S(1)}, u32[]{:S(2)}, u32[]{:S(2)}) %collective-permute-start.5) | collective-permute-done | bytes 1048608 | tf_op jit(solution)/shard_map/ppermute | solution.py:15
  255.9 0.7 fusion.15
  256.6 0.5 fusion.46
  257.3 4.1 collective-permute-start.13
  261.5 0.7 fusion.40
  262.2 34.0 %collective-permute-done.6 = bf16[128,4096]{1,0:T(8,128)(2,1)S(1)} collective-permute-done((bf16[128,4096]{1,0:T(8,128)(2,1)S(1)}, bf16[128,4096]{1,0:T(8,128)(2,1)S(1)}, u32[]{:S(2)}, u32[]{:S(2)}) %collective-permute-start.6) | collective-permute-done | bytes 1048608 | tf_op jit(solution)/shard_map/ppermute | solution.py:15
  296.2 0.7 fusion.16
  296.9 0.5 fusion.47
  298.0 2.7 convolution_add_fusion.1
  300.6 2.6 fusion.52
  303.3 2.6 fusion.51
  305.9 2.7 fusion.50
  308.6 2.7 fusion.49
  311.2 2.6 fusion.48
  313.9 52.7 %collective-permute-done.14 = f32[128,4096]{1,0:T(8,128)} collective-permute-done((f32[128,4096]{1,0:T(8,128)S(1)}, f32[128,4096]{1,0:T(8,128)}, u32[]{:S(2)}, u32[]{:S(2)}) %collective-permute-start.14) | collective-permute-done | bytes 2097184 | tf_op jit(solution)/shard_map/ppermute | solution.py:15
  366.6 11.5 %fusion.39 = (f32[4096]{0:T(1024)S(1)}, bf16[256,4096]{1,0:T(8,128)(2,1)}) fusion(f32[256]{0:T(256)S(1)} %broadcast_add_fusion.1, f32[256,4096]{1,0:T(8,128)} %fusion.48, f32[256,4096]{1,0:T(8,128)} %fusion.49, f32[256,4096]{1,0:T(8,128)} %fusion.50, f32[256,4096]{1,0:T(8,128)} %fusion.51, f32[256,4096]{1,0:T(8,128)} %fusion.52, ...), kind=kOutput, calls=%fused_computation.64 | convolution fusion | flops 285208576 | bytes 30493696 | tf_op jit(solution)/shard_map/dot_general | solution.py:22
  378.1 41.7 %psum.22 = f32[4096]{0:T(1024)S(1)} all-reduce(f32[4096]{0:T(1024)S(1)} %get-tuple-element.5), channel_id=1, replica_groups=mesh['grp'=8,'blk'=32] {'grp'}, use_global_device_ids=true, to_apply=%region_4.0 | all-reduce | flops 4096 | bytes 32768 | tf_op jit(solution)/shard_map/psum | solution.py:9
  419.8 117.4 %psum.23 = f32[4096]{0:T(1024)S(1)} all-reduce(f32[4096]{0:T(1024)S(1)} %psum.22), channel_id=1, replica_groups=mesh['grp'=8,'blk'=32] {'blk'}, use_global_device_ids=true, to_apply=%region_5.0 | all-reduce | flops 4096 | bytes 32768 | tf_op jit(solution)/shard_map/psum | solution.py:9
  537.2 0.6 broadcast_multiply_fusion
  537.8 3.2 fusion.17
  (37 shorter events, 4.0 us)
Async XLA Ops:
  7.2 3.6 copy-start.1
  7.2 2.8 copy-start.3
  7.2 530.6 %all-reduce.2.cloned.1.call-start = ((), (), s32[]{:S(2)}) async-start(), calls=%async_computation | async-start | bytes 4194304 | tf_op jit(solution)/shard_map/psum | solution.py:63
  10.7 1.4 copy-start.2
  11.8 1.6 copy-start
  14.9 40.2 %collective-permute-start.7 = (f32[128,4096]{1,0:T(8,128)S(1)}, f32[128,4096]{1,0:T(8,128)S(1)}, u32[]{:S(2)}, u32[]{:S(2)}) collective-permute-start(f32[128,4096]{1,0:T(8,128)S(1)} %fusion.41), channel_id=1, source_target_pairs={{1,0},{2,1},{3,2},{4,3},{5,4},{6,5},{7,6},{8,7},{9,8},{10,9},{11,1... | collective-permute-start | bytes 6291464 | tf_op jit(solution)/shard_map/ppermute | solution.py:15
  19.5 34.8 %collective-permute-start = (bf16[128,4096]{1,0:T(8,128)(2,1)S(1)}, bf16[128,4096]{1,0:T(8,128)(2,1)S(1)}, u32[]{:S(2)}, u32[]{:S(2)}) collective-permute-start(bf16[128,4096]{1,0:T(8,128)(2,1)S(1)} %fusion.18), channel_id=1, source_target_pairs={{1,0},{2,1},{3,2},{4,3},{5,4},{6,5},{7,6},{8,7},{9,8},{10,9},{11,1... | collective-permute-start | bytes 3145736 | tf_op jit(solution)/shard_map/ppermute | solution.py:15
  55.6 40.1 %collective-permute-start.8 = (f32[128,4096]{1,0:T(8,128)S(1)}, f32[128,4096]{1,0:T(8,128)S(1)}, u32[]{:S(2)}, u32[]{:S(2)}) collective-permute-start(f32[128,4096]{1,0:T(8,128)S(1)} %convolution_add_fusion.2), channel_id=1, source_target_pairs={{1,0},{2,1},{3,2},{4,3},{5,4},{6,5},{7,6},{8,7},{9,8},{10,9},{11,1... | collective-permute-start | bytes 6291464 | tf_op jit(solution)/shard_map/ppermute | solution.py:15
  59.7 34.8 %collective-permute-start.1 = (bf16[128,4096]{1,0:T(8,128)(2,1)S(1)}, bf16[128,4096]{1,0:T(8,128)(2,1)S(1)}, u32[]{:S(2)}, u32[]{:S(2)}) collective-permute-start(bf16[128,4096]{1,0:T(8,128)(2,1)S(1)} %collective-permute-done), channel_id=1, source_target_pairs={{1,0},{2,1},{3,2},{4,3},{5,4},{6,5},{7,6},{8,7},{9,8},{10,9},{11,1... | collective-permute-start | bytes 3145736 | tf_op jit(solution)/shard_map/ppermute | solution.py:15
  95.9 40.1 %collective-permute-start.9 = (f32[128,4096]{1,0:T(8,128)S(1)}, f32[128,4096]{1,0:T(8,128)S(1)}, u32[]{:S(2)}, u32[]{:S(2)}) collective-permute-start(f32[128,4096]{1,0:T(8,128)S(1)} %add.93), channel_id=1, source_target_pairs={{1,0},{2,1},{3,2},{4,3},{5,4},{6,5},{7,6},{8,7},{9,8},{10,9},{11,1... | collective-permute-start | bytes 6291464 | tf_op jit(solution)/shard_map/ppermute | solution.py:15
  100.0 34.8 %collective-permute-start.2 = (bf16[128,4096]{1,0:T(8,128)(2,1)S(1)}, bf16[128,4096]{1,0:T(8,128)(2,1)S(1)}, u32[]{:S(2)}, u32[]{:S(2)}) collective-permute-start(bf16[128,4096]{1,0:T(8,128)(2,1)S(1)} %collective-permute-done.1), channel_id=1, source_target_pairs={{1,0},{2,1},{3,2},{4,3},{5,4},{6,5},{7,6},{8,7},{9,8},{10,9},{11,1... | collective-permute-start | bytes 3145736 | tf_op jit(solution)/shard_map/ppermute | solution.py:15
  136.3 40.1 %collective-permute-start.10 = (f32[128,4096]{1,0:T(8,128)S(1)}, f32[128,4096]{1,0:T(8,128)S(1)}, u32[]{:S(2)}, u32[]{:S(2)}) collective-permute-start(f32[128,4096]{1,0:T(8,128)S(1)} %add.94), channel_id=1, source_target_pairs={{1,0},{2,1},{3,2},{4,3},{5,4},{6,5},{7,6},{8,7},{9,8},{10,9},{11,1... | collective-permute-start | bytes 6291464 | tf_op jit(solution)/shard_map/ppermute | solution.py:15
  140.4 34.8 %collective-permute-start.3 = (bf16[128,4096]{1,0:T(8,128)(2,1)S(1)}, bf16[128,4096]{1,0:T(8,128)(2,1)S(1)}, u32[]{:S(2)}, u32[]{:S(2)}) collective-permute-start(bf16[128,4096]{1,0:T(8,128)(2,1)S(1)} %collective-permute-done.2), channel_id=1, source_target_pairs={{1,0},{2,1},{3,2},{4,3},{5,4},{6,5},{7,6},{8,7},{9,8},{10,9},{11,1... | collective-permute-start | bytes 3145736 | tf_op jit(solution)/shard_map/ppermute | solution.py:15
  176.6 40.1 %collective-permute-start.11 = (f32[128,4096]{1,0:T(8,128)S(1)}, f32[128,4096]{1,0:T(8,128)S(1)}, u32[]{:S(2)}, u32[]{:S(2)}) collective-permute-start(f32[128,4096]{1,0:T(8,128)S(1)} %add.95), channel_id=1, source_target_pairs={{1,0},{2,1},{3,2},{4,3},{5,4},{6,5},{7,6},{8,7},{9,8},{10,9},{11,1... | collective-permute-start | bytes 6291464 | tf_op jit(solution)/shard_map/ppermute | solution.py:15
  180.7 34.8 %collective-permute-start.4 = (bf16[128,4096]{1,0:T(8,128)(2,1)S(1)}, bf16[128,4096]{1,0:T(8,128)(2,1)S(1)}, u32[]{:S(2)}, u32[]{:S(2)}) collective-permute-start(bf16[128,4096]{1,0:T(8,128)(2,1)S(1)} %collective-permute-done.3), channel_id=1, source_target_pairs={{1,0},{2,1},{3,2},{4,3},{5,4},{6,5},{7,6},{8,7},{9,8},{10,9},{11,1... | collective-permute-start | bytes 3145736 | tf_op jit(solution)/shard_map/ppermute | solution.py:15
  217.0 40.1 %collective-permute-start.12 = (f32[128,4096]{1,0:T(8,128)S(1)}, f32[128,4096]{1,0:T(8,128)S(1)}, u32[]{:S(2)}, u32[]{:S(2)}) collective-permute-start(f32[128,4096]{1,0:T(8,128)S(1)} %add.96), channel_id=1, source_target_pairs={{1,0},{2,1},{3,2},{4,3},{5,4},{6,5},{7,6},{8,7},{9,8},{10,9},{11,1... | collective-permute-start | bytes 6291464 | tf_op jit(solution)/shard_map/ppermute | solution.py:15
  221.1 34.8 %collective-permute-start.5 = (bf16[128,4096]{1,0:T(8,128)(2,1)S(1)}, bf16[128,4096]{1,0:T(8,128)(2,1)S(1)}, u32[]{:S(2)}, u32[]{:S(2)}) collective-permute-start(bf16[128,4096]{1,0:T(8,128)(2,1)S(1)} %collective-permute-done.4), channel_id=1, source_target_pairs={{1,0},{2,1},{3,2},{4,3},{5,4},{6,5},{7,6},{8,7},{9,8},{10,9},{11,1... | collective-permute-start | bytes 3145736 | tf_op jit(solution)/shard_map/ppermute | solution.py:15
  257.3 40.1 %collective-permute-start.13 = (f32[128,4096]{1,0:T(8,128)S(1)}, f32[128,4096]{1,0:T(8,128)S(1)}, u32[]{:S(2)}, u32[]{:S(2)}) collective-permute-start(f32[128,4096]{1,0:T(8,128)S(1)} %add.97), channel_id=1, source_target_pairs={{1,0},{2,1},{3,2},{4,3},{5,4},{6,5},{7,6},{8,7},{9,8},{10,9},{11,1... | collective-permute-start | bytes 6291464 | tf_op jit(solution)/shard_map/ppermute | solution.py:15
  261.4 34.8 %collective-permute-start.6 = (bf16[128,4096]{1,0:T(8,128)(2,1)S(1)}, bf16[128,4096]{1,0:T(8,128)(2,1)S(1)}, u32[]{:S(2)}, u32[]{:S(2)}) collective-permute-start(bf16[128,4096]{1,0:T(8,128)(2,1)S(1)} %collective-permute-done.5), channel_id=1, source_target_pairs={{1,0},{2,1},{3,2},{4,3},{5,4},{6,5},{7,6},{8,7},{9,8},{10,9},{11,1... | collective-permute-start | bytes 3145736 | tf_op jit(solution)/shard_map/ppermute | solution.py:15
  297.7 68.9 %collective-permute-start.14 = (f32[128,4096]{1,0:T(8,128)S(1)}, f32[128,4096]{1,0:T(8,128)}, u32[]{:S(2)}, u32[]{:S(2)}) collective-permute-start(f32[128,4096]{1,0:T(8,128)S(1)} %add.98), channel_id=1, source_target_pairs={{25,0},{26,1},{27,2},{28,3},{29,4},{30,5},{31,6},{0,7},{1,8},{2,9}... | collective-permute-start | bytes 6291464 | tf_op jit(solution)/shard_map/ppermute | solution.py:15
Sparse Core Ops, SparseCore 0:
  366.7 128.9 all-reduce.1
